TPU v7x, 512 devices: a whole 4x4x16 slice. The times are simulated.
512 devices in a mesh: space: 64 (over z, x_hi, core), scen: 8 (over x_lo, y).
Axes of the slice: x: 4 (x_hi: 2, x_lo: 2; x = x_hi * 2 + x_lo), y: 4, z: 16, core: 2. Of those that a mesh axis runs over, the one named last changes fastest.
Arguments:
- dwell_map: bfloat16 [16384, 1024], P('space', 'scen'), may hold values from 0 to 1
- target_map: bfloat16 [16384, 1024], P('space'), may hold values from -6 to 6
- bound_mask: int32 [16384, 1024], P('space', 'scen'), may hold values 0 or 1
- offsets: int32 [16, 2], replicated, may hold values from -32 to 32, as said below
- rate_index: int32 [16, 1], replicated, may hold values from 0 to 3
- rate_table: float32 [4], replicated, may hold values from 0.5 to 2
- row_kernels: bfloat16 [4, 63], replicated, may hold values from -0.75 to 0.75
- col_kernels: bfloat16 [4, 63], replicated, may hold values from -0.75 to 0.75
Outputs:
- dwell_next: bfloat16 [16384, 1024], P('space', 'scen')
Inputs may be any that keep to these rules, and one draw needn't show every extreme that they name: `offsets`: each entry lies between -32 and 32; in each column some scenario has 32 and another -32. `rate_index`: every level is used by some scenario.
All inputs are finite; a program needn't handle non-finite values. No bound on the sum of `bound_mask` on one device may be relied on, other than what follows from the above.
Results may differ from a plain program's by a relative error of at most 0.014.
Values may be sent and summed in bfloat16 or wider, within the bound.
A program may use at most 64 MiB of HBM per device.

v0:
```python
import jax
import jax.numpy as jnp
from jax import lax
from jax.sharding import PartitionSpec as P

S_DEV = 2
KTAPS = 63
REACH = 32
step_size = 1.0


def extended(x, sides, width):
    for axis, dim in sides:
        count, length = (lax.axis_size(axis), x.shape[dim])
        up = [(i, (i + 1) % count) for i in range(count - 1)]
        down = [(j, i) for i, j in up]
        last = lax.slice_in_dim(x, length - width, length, axis=dim)
        first = lax.slice_in_dim(x, 0, width, axis=dim)
        before = lax.ppermute(last, axis, up)
        after = lax.ppermute(first, axis, down)
        x = jnp.concatenate([before, x, after], axis=dim)
    return x


def band_line(kernel, start_at, row_count, col_count):
    kernel_line = jnp.zeros((col_count + 1,), kernel.dtype)
    kernel_line = lax.dynamic_update_slice(kernel_line, kernel, (start_at,))
    return jnp.tile(kernel_line, row_count)[: row_count * col_count].reshape(row_count, col_count)


def column_pass(values, kernels, shifts):
    scen_count, height, col_total = values.shape
    col_block = 128
    padded = jnp.pad(values, ((0, 0), (0, 0), (col_block, col_block)))

    def column_one_band(kernel, shift):
        return band_line(kernel, shift + col_block, col_block, 3 * col_block)

    matrices = jax.vmap(column_one_band)(kernels, shifts)
    product = jnp.zeros((scen_count, height, col_total // col_block, col_block), jnp.float32)
    for piece in range(3):
        view = padded[:, :, piece * col_block : piece * col_block + col_total].reshape(
            scen_count, height, col_total // col_block, col_block
        )
        part_mat = matrices[:, :, piece * col_block : (piece + 1) * col_block]
        product = product + jnp.einsum(
            "srny,scy->srnc", view, part_mat, preferred_element_type=jnp.float32
        )
    return product.reshape(scen_count, height, col_total)


def row_pass(values, kernels, shifts, out_rows):
    in_rows = values.shape[-2]
    rim_depth = (in_rows - out_rows) // 2
    row_block = 128
    block_count = -(-out_rows // row_block)
    window = row_block + 2 * rim_depth
    if values.ndim == 2:
        padded = values
    else:
        padded = values

    def row_one_band(kernel, shift):
        return band_line(kernel, shift + rim_depth, row_block, window)

    matrices = jax.vmap(row_one_band)(kernels, shifts)
    results = []
    for block_id in range(block_count):
        begin = block_id * row_block
        if values.ndim == 2:
            view = padded[begin : begin + window]
            results.append(
                jnp.einsum("sie,ew->siw", matrices, view, preferred_element_type=jnp.float32)
            )
        else:
            view = padded[:, begin : begin + window]
            results.append(
                jnp.einsum("sie,sew->siw", matrices, view, preferred_element_type=jnp.float32)
            )
    return jnp.concatenate(results, axis=1)


def shards(
    dwell_map, target_map, bound_mask, offsets, rate_index, rate_table, row_kernels, col_kernels
):
    tile_rows = dwell_map.shape[0]
    radius = (KTAPS - 1) // 2
    halo_rows = REACH + radius
    scen_count = S_DEV * lax.axis_size("scen")
    first_scen = lax.axis_index("scen") * S_DEV
    my_offsets = lax.dynamic_slice_in_dim(offsets, first_scen, S_DEV, 0)
    shift_rows = my_offsets[:, 0]
    shift_cols = my_offsets[:, 1]
    level_ids = lax.dynamic_slice_in_dim(rate_index, first_scen, S_DEV, 0)[:, 0]
    onehot = (
        level_ids[:, None] == jnp.arange(rate_table.shape[0], dtype=jnp.int32)[None, :]
    ).astype(jnp.float32)
    my_rates = jnp.sum(onehot * rate_table[None, :], axis=1)
    my_row_taps = jnp.sum(
        onehot[:, :, None] * row_kernels.astype(jnp.float32)[None], axis=1
    ).astype(jnp.bfloat16)
    my_col_taps = jnp.sum(
        onehot[:, :, None] * col_kernels.astype(jnp.float32)[None], axis=1
    ).astype(jnp.bfloat16)
    full_map = lax.all_gather(dwell_map, "scen", axis=1, tiled=True)
    rim_rows = extended(full_map, (("space", 0),), halo_rows)
    forward = row_pass(rim_rows, my_row_taps, -radius - shift_rows, tile_rows).astype(jnp.bfloat16)
    removal = my_rates[:, None, None] * column_pass(forward, my_col_taps, -radius - shift_cols)
    misfit = (removal - target_map.astype(jnp.float32)[None]).astype(jnp.bfloat16)
    misfit_rows = extended(misfit, (("space", 1),), halo_rows)
    back_cols = column_pass(misfit_rows, my_col_taps[:, ::-1], -radius + shift_cols).astype(
        jnp.bfloat16
    )
    adjoint = row_pass(back_cols, my_row_taps[:, ::-1], -radius + shift_rows, tile_rows)
    group_sum = jnp.sum((my_rates / scen_count)[:, None, None] * adjoint, axis=0)
    gradient = lax.psum_scatter(
        group_sum.astype(jnp.bfloat16), "scen", scatter_dimension=1, tiled=True
    ).astype(jnp.float32)
    stepped = dwell_map.astype(jnp.float32) - step_size * gradient
    return jnp.where(bound_mask == 1, jnp.maximum(stepped, 0.0), stepped).astype(jnp.bfloat16)


def solution(mesh):
    return jax.shard_map(
        shards,
        mesh=mesh,
        in_specs=(
            P("space", "scen"),
            P("space", None),
            P("space", "scen"),
            P(),
            P(),
            P(),
            P(),
            P(),
        ),
        out_specs=P("space", "scen"),
        check_vma=False,
    )
```

profile of v0, /device:TPU:32, one launch (start us, length us, event | category | flops | bytes accessed | tf_op | source)
XLA Modules:
  0.0 196.9 jit_solution(3160482951217890527)
XLA Ops:
  6.5 26.4 %all_gather.3 = bf16[256,1024]{1,0:T(8,128)(2,1)S(1)} all-gather(bf16[256,128]{1,0:T(8,128)(2,1)} %param.8), channel_id=1, replica_groups=mesh['space'=64,'scen'=8] {'scen'}, dimensions={1}, use_global_device_ids=true | all-gather | bytes 589824 | tf_op jit(solution)/shard_map/all_gather | solution.py:105
  33.0 1.9 collective-permute-start
  34.9 6.0 %collective-permute-start.1 = (bf16[63,1024]{1,0:T(8,128)(2,1)S(1)}, bf16[63,1024]{1,0:T(8,128)(2,1)S(1)}, u32[]{:S(2)}, u32[]{:S(2)}) collective-permute-start(bf16[63,1024]{1,0:T(8,128)(2,1)S(1)} %get-tuple-element.86), channel_id=1, source_target_pairs={{8,0},{16,8},{24,16},{32,24},{40,32},{48,40},{56,48},{64,56},{72,6... | collective-permute-start | bytes 387080 | tf_op jit(solution)/shard_map/ppermute | solution.py:20
  41.3 0.7 dynamic-slice_bitcast_fusion
  42.1 0.7 convert_element_type.51
  42.7 0.7 convert_element_type.53
  43.6 13.4 %while.5 = (s32[]{:T(128)}, bf16[2,255]{1,0:T(2,128)(2,1)S(1)}, s32[2,2]{1,0:T(2,128)S(1)}, bf16[2,63]{1,0:T(2,128)(2,1)S(1)}, s32[]{:T(128)}, /*index=5*/s32[2]{0:T(128)}) while((s32[]{:T(128)}, bf16[2,255]{1,0:T(2,128)(2,1)S(1)}, s32[2,2]{1,0:T(2,128)S(1)}, bf16[2,63]{1,0:T(2,128)(2,1)S(1)}, s32[]{:T(128)}, /*index=5*/s32[2]{0:T(128)}) %tuple.77), condition=%wide.while_cond.1, body=%wide.while_body.1.sunk | while | flops 74 | bytes 769 | solution.py:27
  43.6 0.6 fusion.58
  44.2 2.7 %and_reduce_fusion.9 = pred[]{:T(512)} fusion(s32[2]{0:T(128)} %get-tuple-element.250, s32[1]{0:T(128)} %bitcast.121, s32[1]{0:T(128)} %bitcast.122), kind=kLoop, calls=%fused_computation.3.clone.1 | loop fusion | flops 9 | bytes 17 | tf_op jit(solution)/shard_map/vmap(vmap())/scatter
  46.9 2.0 broadcast_select_fusion.9
  48.8 1.4 dynamic-update-slice.9
  50.3 0.6 fusion.58
  50.9 2.7 %and_reduce_fusion.9 = pred[]{:T(512)} fusion(s32[2]{0:T(128)} %get-tuple-element.250, s32[1]{0:T(128)} %bitcast.121, s32[1]{0:T(128)} %bitcast.122), kind=kLoop, calls=%fused_computation.3.clone.1 | loop fusion | flops 9 | bytes 17 | tf_op jit(solution)/shard_map/vmap(vmap())/scatter
  53.5 2.0 broadcast_select_fusion.9
  55.5 1.6 dynamic-update-slice.9
  57.2 13.7 %while.6 = (s32[]{:T(128)}, bf16[2,385]{1,0:T(2,128)(2,1)S(1)}, s32[2,2]{1,0:T(2,128)S(1)}, bf16[2,63]{1,0:T(2,128)(2,1)S(1)}, s32[]{:T(128)}, /*index=5*/s32[2]{0:T(128)}) while((s32[]{:T(128)}, bf16[2,385]{1,0:T(2,128)(2,1)S(1)}, s32[2,2]{1,0:T(2,128)S(1)}, bf16[2,63]{1,0:T(2,128)(2,1)S(1)}, s32[]{:T(128)}, /*index=5*/s32[2]{0:T(128)}) %tuple.80), condition=%wide.while_cond.2, body=%wide.while_body.2.sunk | while | flops 74 | bytes 769 | solution.py:27
  57.2 0.6 fusion.59
  57.8 2.7 %and_reduce_fusion.10 = pred[]{:T(512)} fusion(s32[2]{0:T(128)} %get-tuple-element.268, s32[1]{0:T(128)} %bitcast.125, s32[1]{0:T(128)} %bitcast.126), kind=kLoop, calls=%fused_computation.6.clone.1 | loop fusion | flops 9 | bytes 17 | tf_op jit(solution)/shard_map/vmap(vmap())/scatter
  60.5 2.0 %broadcast_select_fusion.10 = bf16[1,63]{1,0:T(2,128)(2,1)S(1)} fusion(pred[]{:T(512)} %and_reduce_fusion.10, bf16[2,63]{1,0:T(2,128)(2,1)S(1)} %get-tuple-element.266, s32[]{:T(128)} %get-tuple-element.257, bf16[2,385]{1,0:T(2,128)(2,1)S(1)} %get-tuple-element.258, s32[]{:T(128)} %bitcast.127, s32[]{:T(128)} %bitcast.128), kind=kLoop, calls=%fused_computation.7.clone.1 | loop fusion | flops 63 | bytes 391 | tf_op jit(solution)/shard_map/vmap(vmap())/scatter
  62.5 1.6 dynamic-update-slice.10
  64.0 0.6 fusion.59
  64.6 2.7 %and_reduce_fusion.10 = pred[]{:T(512)} fusion(s32[2]{0:T(128)} %get-tuple-element.268, s32[1]{0:T(128)} %bitcast.125, s32[1]{0:T(128)} %bitcast.126), kind=kLoop, calls=%fused_computation.6.clone.1 | loop fusion | flops 9 | bytes 17 | tf_op jit(solution)/shard_map/vmap(vmap())/scatter
  67.3 2.0 %broadcast_select_fusion.10 = bf16[1,63]{1,0:T(2,128)(2,1)S(1)} fusion(pred[]{:T(512)} %and_reduce_fusion.10, bf16[2,63]{1,0:T(2,128)(2,1)S(1)} %get-tuple-element.266, s32[]{:T(128)} %get-tuple-element.257, bf16[2,385]{1,0:T(2,128)(2,1)S(1)} %get-tuple-element.258, s32[]{:T(128)} %bitcast.127, s32[]{:T(128)} %bitcast.128), kind=kLoop, calls=%fused_computation.7.clone.1 | loop fusion | flops 63 | bytes 391 | tf_op jit(solution)/shard_map/vmap(vmap())/scatter
  69.3 1.6 dynamic-update-slice.10
  70.9 13.5 %while.7 = (s32[]{:T(128)}, bf16[2,385]{1,0:T(2,128)(2,1)S(1)}, s32[2,2]{1,0:T(2,128)S(1)}, bf16[2,63]{1,0:T(2,128)(2,1)S(1)}, s32[]{:T(128)}, /*index=5*/s32[2]{0:T(128)}) while((s32[]{:T(128)}, bf16[2,385]{1,0:T(2,128)(2,1)S(1)}, s32[2,2]{1,0:T(2,128)S(1)}, bf16[2,63]{1,0:T(2,128)(2,1)S(1)}, s32[]{:T(128)}, /*index=5*/s32[2]{0:T(128)}) %tuple.89), condition=%wide.while_cond.3, body=%wide.while_body.3.sunk | while | flops 74 | bytes 769 | solution.py:27
  71.0 0.7 fusion.60
  71.6 2.6 %and_reduce_fusion.11 = pred[]{:T(512)} fusion(s32[2]{0:T(128)} %get-tuple-element.286, s32[1]{0:T(128)} %bitcast.129, s32[1]{0:T(128)} %bitcast.130), kind=kLoop, calls=%fused_computation.9.clone.1 | loop fusion | flops 9 | bytes 17 | tf_op jit(solution)/shard_map/vmap(vmap())/scatter
  74.2 1.9 broadcast_select_fusion.11
  76.1 1.6 dynamic-update-slice.11
  77.7 0.7 fusion.60
  78.4 2.6 %and_reduce_fusion.11 = pred[]{:T(512)} fusion(s32[2]{0:T(128)} %get-tuple-element.286, s32[1]{0:T(128)} %bitcast.129, s32[1]{0:T(128)} %bitcast.130), kind=kLoop, calls=%fused_computation.9.clone.1 | loop fusion | flops 9 | bytes 17 | tf_op jit(solution)/shard_map/vmap(vmap())/scatter
  81.0 1.9 broadcast_select_fusion.11
  82.9 1.6 dynamic-update-slice.11
  84.5 0.5 tile.19
  85.6 0.7 tile.41
  90.1 1.0 fusion.41
  91.1 1.9 collective-permute-start.2
  93.0 6.2 %collective-permute-start.3 = (bf16[2,63,1024]{1,2,0:T(8,128)(2,1)S(1)}, bf16[2,63,1024]{1,2,0:T(8,128)(2,1)}, u32[]{:S(2)}, u32[]{:S(2)}) collective-permute-start(bf16[2,63,1024]{1,2,0:T(8,128)(2,1)S(1)} %get-tuple-element.84), channel_id=1, source_target_pairs={{8,0},{16,8},{24,16},{32,24},{40,32},{48,40},{56,48},{64,56},{72,6... | collective-permute-start | bytes 774152 | tf_op jit(solution)/shard_map/ppermute | solution.py:20
  99.3 12.7 %while.4 = (s32[]{:T(128)}, bf16[2,255]{1,0:T(2,128)(2,1)S(1)}, s32[2,2]{1,0:T(2,128)S(1)}, bf16[2,63]{1,0:T(2,128)(2,1)S(1)}, s32[]{:T(128)}, /*index=5*/s32[2]{0:T(128)S(1)}) while((s32[]{:T(128)}, bf16[2,255]{1,0:T(2,128)(2,1)S(1)}, s32[2,2]{1,0:T(2,128)S(1)}, bf16[2,63]{1,0:T(2,128)(2,1)S(1)}, s32[]{:T(128)}, /*index=5*/s32[2]{0:T(128)S(1)}) %tuple.88), condition=%wide.while_cond, body=%wide.while_body.sunk | while | flops 74 | bytes 769 | solution.py:27
  99.3 0.6 fusion.57
  100.0 2.0 %and_reduce_fusion.8 = pred[]{:T(512)} fusion(s32[2]{0:T(128)S(1)} %get-tuple-element.232, s32[1]{0:T(128)} %bitcast.117, s32[1]{0:T(128)} %bitcast.118), kind=kLoop, calls=%fused_computation.clone.1 | loop fusion | flops 9 | bytes 17 | tf_op jit(solution)/shard_map/vmap(vmap())/scatter
  102.0 2.0 %broadcast_select_fusion.8 = bf16[1,63]{1,0:T(2,128)(2,1)S(1)} fusion(pred[]{:T(512)} %and_reduce_fusion.8, bf16[2,63]{1,0:T(2,128)(2,1)S(1)} %get-tuple-element.230, s32[]{:T(128)} %get-tuple-element.221, bf16[2,255]{1,0:T(2,128)(2,1)S(1)} %get-tuple-element.222, s32[]{:T(128)} %bitcast.119, s32[]{:T(128)} %bitcast.120), kind=kLoop, calls=%fused_computation.1.clone.1 | loop fusion | flops 63 | bytes 391 | tf_op jit(solution)/shard_map/vmap(vmap())/scatter
  104.0 1.6 dynamic-update-slice.8
  105.6 0.6 fusion.57
  106.3 2.0 %and_reduce_fusion.8 = pred[]{:T(512)} fusion(s32[2]{0:T(128)S(1)} %get-tuple-element.232, s32[1]{0:T(128)} %bitcast.117, s32[1]{0:T(128)} %bitcast.118), kind=kLoop, calls=%fused_computation.clone.1 | loop fusion | flops 9 | bytes 17 | tf_op jit(solution)/shard_map/vmap(vmap())/scatter
  108.3 2.0 %broadcast_select_fusion.8 = bf16[1,63]{1,0:T(2,128)(2,1)S(1)} fusion(pred[]{:T(512)} %and_reduce_fusion.8, bf16[2,63]{1,0:T(2,128)(2,1)S(1)} %get-tuple-element.230, s32[]{:T(128)} %get-tuple-element.221, bf16[2,255]{1,0:T(2,128)(2,1)S(1)} %get-tuple-element.222, s32[]{:T(128)} %bitcast.119, s32[]{:T(128)} %bitcast.120), kind=kLoop, calls=%fused_computation.1.clone.1 | loop fusion | flops 63 | bytes 391 | tf_op jit(solution)/shard_map/vmap(vmap())/scatter
  110.3 1.6 dynamic-update-slice.8
  112.0 0.7 tile.43
  112.9 0.5 tile.17
  114.0 0.8 copy-done.3
  114.8 2.2 %pad_maximum_fusion = bf16[2,382,1024]{1,2,0:T(8,128)(2,1)S(1)} fusion(bf16[2,63,1024]{1,2,0:T(8,128)(2,1)} %collective-permute-done.3, bf16[2,256,1024]{1,2,0:T(8,128)(2,1)S(1)} %fusion.3, bf16[2,63,1024]{1,2,0:T(8,128)(2,1)} %copy-done.3), kind=kLoop, calls=%fused_computation.26 | loop fusion | flops 4694016 | bytes 3129344 | tf_op jit(solution)/shard_map/concatenate | solution.py:21
  116.9 1.5 pad_slice_fusion.1
  118.4 2.9 %copy.48 = bf16[2,382,8,128]{3,2,1,0:T(8,128)(2,1)} copy(bf16[2,382,8,128]{1,3,2,0:T(8,128)(2,1)} %bitcast.137) | data formatting | bytes 3129344 | tf_op jit(solution)/shard_map/reshape | solution.py:42
  121.4 2.0 %copy.50 = bf16[2,382,8,128]{3,2,1,0:T(8,128)(2,1)} copy(bf16[2,382,8,128]{1,3,2,0:T(8,128)(2,1)S(1)} %bitcast.136) | data formatting | bytes 3129344 | tf_op jit(solution)/shard_map/reshape | solution.py:42
  123.4 3.7 %fusion.28 = f32[2,382,8,128]{3,2,1,0:T(8,128)} fusion(bf16[2,382,8,128]{3,2,1,0:T(8,128)(2,1)} %copy.48, bf16[2,128,384]{2,1,0:T(8,128)(2,1)S(1)} %bitcast.139), kind=kOutput, calls=%fused_computation.61 | convolution fusion | flops 200278016 | bytes 4759552 | tf_op jit(solution)/shard_map/srny,scy->srnc/dot_general | solution.py:46
  127.1 2.2 %fusion.27 = f32[2,382,8,128]{3,2,1,0:T(8,128)} fusion(bf16[2,382,8,128]{3,2,1,0:T(8,128)(2,1)S(1)} %copy-done.1, bf16[2,128,384]{2,1,0:T(8,128)(2,1)S(1)} %bitcast.140), kind=kOutput, calls=%fused_computation.58 | convolution fusion | flops 200278016 | bytes 4759552 | tf_op jit(solution)/shard_map/srny,scy->srnc/dot_general | solution.py:46
  129.4 1.2 copy.49
  130.6 4.7 %add_convert_fusion = bf16[2,382,8,128]{3,2,1,0:T(8,128)(2,1)} fusion(f32[2,382,8,128]{3,2,1,0:T(8,128)} %fusion.27, f32[2,382,8,128]{3,2,1,0:T(8,128)} %fusion.28, bf16[2,382,8,128]{3,2,1,0:T(8,128)(2,1)S(1)} %copy.49, bf16[2,128,384]{2,1,0:T(8,128)(2,1)S(1)} %bitcast.141), kind=kOutput, calls=%fused_computation.14 | convolution fusion | flops 202625024 | bytes 9453568 | tf_op jit(solution)/shard_map/srny,scy->srnc/dot_general | solution.py:46
  135.2 2.1 %copy.51 = bf16[2,382,8,128]{1,3,2,0:T(8,128)(2,1)S(1)} copy(bf16[2,382,8,128]{3,2,1,0:T(8,128)(2,1)} %add_convert_fusion) | data formatting | bytes 3129344 | tf_op jit(solution)/shard_map/convert_element_type | solution.py:111
  137.8 0.5 fusion.12
  138.7 1.0 copy.60
  139.7 48.7 %reduce-scatter.4.cloned.1.call-done = bf16[128,256]{1,0:T(8,128)(2,1)} async-done(((bf16[1024,256]{1,0:T(8,128)(2,1)}), bf16[128,256]{1,0:T(8,128)(2,1)}) %reduce-scatter.4.cloned.1.call-update) | async-done | bytes 65552
  188.4 0.9 copy.61
  189.4 0.7 fusion.26
  (72 shorter events, 6.6 us)
Async XLA Ops:
  6.5 34.5 %copy-start = (s32[16,2]{0,1:T(2,128)S(1)}, s32[16,2]{0,1:T(2,128)}, u32[]{:S(2)}) copy-start(s32[16,2]{0,1:T(2,128)} %param.11) | copy-start | bytes 388
  6.5 80.0 %copy-start.2 = (bf16[256,1024]{1,0:T(8,128)(2,1)S(1)}, bf16[256,1024]{1,0:T(8,128)(2,1)}, u32[]{:S(2)}) copy-start(bf16[256,1024]{1,0:T(8,128)(2,1)} %param.9) | copy-start | bytes 1572868
  6.5 181.8 %reduce-scatter.4.cloned.1.call-start = ((), (), s32[]{:S(2)}) async-start(), calls=%async_computation.1 | async-start | bytes 589824
  33.0 53.9 %collective-permute-start = (bf16[63,1024]{1,0:T(8,128)(2,1)S(1)}, bf16[63,1024]{1,0:T(8,128)(2,1)S(1)}, u32[]{:S(2)}, u32[]{:S(2)}) collective-permute-start(bf16[63,1024]{1,0:T(8,128)(2,1)S(1)} %get-tuple-element.85), channel_id=1, source_target_pairs={{0,8},{8,16},{16,24},{24,32},{32,40},{40,48},{48,56},{56,64},{64,7... | collective-permute-start | bytes 387080 | tf_op jit(solution)/shard_map/ppermute | solution.py:19
  34.9 52.4 %collective-permute-start.1 = (bf16[63,1024]{1,0:T(8,128)(2,1)S(1)}, bf16[63,1024]{1,0:T(8,128)(2,1)S(1)}, u32[]{:S(2)}, u32[]{:S(2)}) collective-permute-start(bf16[63,1024]{1,0:T(8,128)(2,1)S(1)} %get-tuple-element.86), channel_id=1, source_target_pairs={{8,0},{16,8},{24,16},{32,24},{40,32},{48,40},{56,48},{64,56},{72,6... | collective-permute-start | bytes 387080 | tf_op jit(solution)/shard_map/ppermute | solution.py:20
  70.9 15.8 %copy-start.7 = (f32[4]{0:T(128)S(1)}, f32[4]{0:T(128)}, u32[]{:S(2)}) copy-start(f32[4]{0:T(128)} %param.13) | copy-start | bytes 52
  90.1 9.2 %copy-start.6 = (s32[2]{0:T(128)S(1)}, s32[2]{0:T(128)}, u32[]{:S(2)}) copy-start(s32[2]{0:T(128)} %get-tuple-element.297) | copy-start | bytes 28
  91.1 22.8 %collective-permute-start.2 = (bf16[2,63,1024]{1,2,0:T(8,128)(2,1)}, bf16[2,63,1024]{1,2,0:T(8,128)(2,1)S(1)}, u32[]{:S(2)}, u32[]{:S(2)}) collective-permute-start(bf16[2,63,1024]{1,2,0:T(8,128)(2,1)} %get-tuple-element.83), channel_id=1, source_target_pairs={{0,8},{8,16},{16,24},{24,32},{32,40},{40,48},{48,56},{56,64},{64,7... | collective-permute-start | bytes 774152 | tf_op jit(solution)/shard_map/ppermute | solution.py:19
  93.0 21.7 %collective-permute-start.3 = (bf16[2,63,1024]{1,2,0:T(8,128)(2,1)S(1)}, bf16[2,63,1024]{1,2,0:T(8,128)(2,1)}, u32[]{:S(2)}, u32[]{:S(2)}) collective-permute-start(bf16[2,63,1024]{1,2,0:T(8,128)(2,1)S(1)} %get-tuple-element.84), channel_id=1, source_target_pairs={{8,0},{16,8},{24,16},{32,24},{40,32},{48,40},{56,48},{64,56},{72,6... | collective-permute-start | bytes 774152 | tf_op jit(solution)/shard_map/ppermute | solution.py:20
  114.0 0.8 copy-start.3
  123.4 3.7 %copy-start.1 = (bf16[2,382,8,128]{3,2,1,0:T(8,128)(2,1)S(1)}, bf16[2,382,8,128]{3,2,1,0:T(8,128)(2,1)}, u32[]{:S(2)}) copy-start(bf16[2,382,8,128]{3,2,1,0:T(8,128)(2,1)} %copy.50) | copy-start | bytes 4694020
  138.3 51.0 %copy-start.4 = (bf16[256,128]{1,0:T(8,128)(2,1)S(1)}, bf16[256,128]{1,0:T(8,128)(2,1)}, u32[]{:S(2)}) copy-start(bf16[256,128]{1,0:T(8,128)(2,1)} %param.8) | copy-start | bytes 196612
  138.3 51.0 %copy-start.5 = (s32[256,128]{1,0:T(8,128)S(1)}, s32[256,128]{1,0:T(8,128)}, u32[]{:S(2)}) copy-start(s32[256,128]{1,0:T(8,128)} %param.10) | copy-start | bytes 393220
Sparse Core Ops, SparseCore 0:
  139.8 48.5 reduce-scatter.3
where the time goes:
time: 198 us; the launch traced here: 197 us
  waiting for transfers between devices  48.7 us (25%)
  other arithmetic  41.2 us (21%)
  local copies, waits for them, and re-layouts  36.8 us (19%)
  blocking collectives  26.4 us (13%)
  starting transfers between devices  16.1 us (8%)
  between operations  13.8 us (7%)
  matrix products  13.6 us (7%)
    unnamed x2, waiting for transfers between devices  48.7 us
    scatter x16, other arithmetic  35.7 us
    all_gather x1, blocking collectives, shards(): full_map = lax.all_gather(dwell_map, 'scen', axis=1, tiled=True)  26.4 us
    scatter x24, local copies, waits for them, and re-layouts  17.4 us
    ppermute x2, starting transfers between devices, extended(): after = lax.ppermute(first, axis, down)  12.3 us
    dot_general x6, matrix products, column_pass(): jnp.einsum('srny,scy->srnc', view, part_mat, preferred_element_type=jnp.f...  12 us
    reshape x3, local copies, waits for them, and re-layouts, column_pass(): padded[:, :, piece * col_block:piece * col_block + col_total]  6.16 us
  transfers between devices with their start and end apart: 5, of which 1 were waited for; matrix products, arithmetic and copies ran while one was open for 31% of the time, Pallas kernels for 0%

commit v1 on v0

--- a/solution.py
+++ b/solution.py
@@ -102,7 +102,9 @@
     my_col_taps = jnp.sum(
         onehot[:, :, None] * col_kernels.astype(jnp.float32)[None], axis=1
     ).astype(jnp.bfloat16)
-    full_map = lax.all_gather(dwell_map, "scen", axis=1, tiled=True)
+    full_map = jnp.concatenate(
+        lax.all_to_all(jnp.stack([dwell_map] * lax.axis_size("scen")), "scen", 0, 0), axis=1
+    )
     rim_rows = extended(full_map, (("space", 0),), halo_rows)
     forward = row_pass(rim_rows, my_row_taps, -radius - shift_rows, tile_rows).astype(jnp.bfloat16)
     removal = my_rates[:, None, None] * column_pass(forward, my_col_taps, -radius - shift_cols)

time: 198 us -> 183 us (0.924)
  the two profiles are of different devices: /device:TPU:32 before, /device:TPU:4 now
where the time goes in v1:
time: 183 us; the launch traced here: 182 us
  waiting for transfers between devices  55 us (30%)
  other arithmetic  40.8 us (22%)
  local copies, waits for them, and re-layouts  38.8 us (21%)
  starting transfers between devices  19.7 us (11%)
  between operations  13.9 us (8%)
  matrix products  13.6 us (7%)
    unnamed x2, waiting for transfers between devices  53 us
    scatter x16, other arithmetic  35.3 us
    scatter x24, local copies, waits for them, and re-layouts  17.3 us
    dot_general x6, matrix products, column_pass(): jnp.einsum('srny,scy->srnc', view, part_mat, preferred_element_type=jnp.f...  12 us
    ppermute x2, starting transfers between devices, extended(): after = lax.ppermute(first, axis, down)  7.33 us
    ppermute x2, starting transfers between devices, extended(): before = lax.ppermute(last, axis, up)  7.1 us
    reshape x3, local copies, waits for them, and re-layouts, column_pass(): padded[:, :, piece * col_block:piece * col_block + col_total]  6.15 us
    all_to_all x1, starting transfers between devices, shards(): lax.all_to_all(jnp.stack([dwell_map] * lax.axis_size('scen')), 'scen', 0, 0)  5.24 us
  transfers between devices with their start and end apart: 6, of which 3 were waited for; matrix products, arithmetic and copies ran while one was open for 33% of the time, Pallas kernels for 0%

profile of v1, /device:TPU:4, one launch (start us, length us, event | category | flops | bytes accessed | tf_op | source)
XLA Modules:
  0.0 182.0 jit_solution(2148863904584651767)
XLA Ops:
  6.5 1.7 stack.2
  8.3 5.2 %all-to-all-start = ((bf16[8,256,128]{2,1,0:T(8,128)(2,1)}), bf16[8,256,128]{2,1,0:T(8,128)(2,1)S(1)}, u32[]{:S(2)}, u32[]{:S(2)}) async-start(bf16[8,256,128]{2,1,0:T(8,128)(2,1)} %stack.2), calls=%async_computation | async-start | bytes 1048576 | tf_op jit(solution)/shard_map/all_to_all | solution.py:106
  13.8 0.7 dynamic-slice_bitcast_fusion
  14.6 0.7 convert_element_type.51
  15.3 0.7 convert_element_type.53
  16.2 13.5 %while.5 = (s32[]{:T(128)}, bf16[2,255]{1,0:T(2,128)(2,1)S(1)}, s32[2,2]{1,0:T(2,128)S(1)}, bf16[2,63]{1,0:T(2,128)(2,1)S(1)}, s32[]{:T(128)}, /*index=5*/s32[2]{0:T(128)}) while((s32[]{:T(128)}, bf16[2,255]{1,0:T(2,128)(2,1)S(1)}, s32[2,2]{1,0:T(2,128)S(1)}, bf16[2,63]{1,0:T(2,128)(2,1)S(1)}, s32[]{:T(128)}, /*index=5*/s32[2]{0:T(128)}) %tuple.77), condition=%wide.while_cond.1, body=%wide.while_body.1.sunk | while | flops 74 | bytes 769 | solution.py:27
  16.2 0.6 fusion.59
  16.8 2.7 %and_reduce_fusion.9 = pred[]{:T(512)} fusion(s32[2]{0:T(128)} %get-tuple-element.250, s32[1]{0:T(128)} %bitcast.133, s32[1]{0:T(128)} %bitcast.134), kind=kLoop, calls=%fused_computation.3.clone.1 | loop fusion | flops 9 | bytes 17 | tf_op jit(solution)/shard_map/vmap(vmap())/scatter
  19.4 2.0 %broadcast_select_fusion.9 = bf16[1,63]{1,0:T(2,128)(2,1)S(1)} fusion(pred[]{:T(512)} %and_reduce_fusion.9, bf16[2,63]{1,0:T(2,128)(2,1)S(1)} %get-tuple-element.248, s32[]{:T(128)} %get-tuple-element.239, bf16[2,255]{1,0:T(2,128)(2,1)S(1)} %get-tuple-element.240, s32[]{:T(128)} %bitcast.135, s32[]{:T(128)} %bitcast.136), kind=kLoop, calls=%fused_computation.4.clone.1 | loop fusion | flops 63 | bytes 391 | tf_op jit(solution)/shard_map/vmap(vmap())/scatter
  21.4 1.4 dynamic-update-slice.9
  22.9 0.6 fusion.59
  23.5 2.7 %and_reduce_fusion.9 = pred[]{:T(512)} fusion(s32[2]{0:T(128)} %get-tuple-element.250, s32[1]{0:T(128)} %bitcast.133, s32[1]{0:T(128)} %bitcast.134), kind=kLoop, calls=%fused_computation.3.clone.1 | loop fusion | flops 9 | bytes 17 | tf_op jit(solution)/shard_map/vmap(vmap())/scatter
  26.1 2.0 %broadcast_select_fusion.9 = bf16[1,63]{1,0:T(2,128)(2,1)S(1)} fusion(pred[]{:T(512)} %and_reduce_fusion.9, bf16[2,63]{1,0:T(2,128)(2,1)S(1)} %get-tuple-element.248, s32[]{:T(128)} %get-tuple-element.239, bf16[2,255]{1,0:T(2,128)(2,1)S(1)} %get-tuple-element.240, s32[]{:T(128)} %bitcast.135, s32[]{:T(128)} %bitcast.136), kind=kLoop, calls=%fused_computation.4.clone.1 | loop fusion | flops 63 | bytes 391 | tf_op jit(solution)/shard_map/vmap(vmap())/scatter
  28.1 1.6 dynamic-update-slice.9
  29.8 13.5 %while.6 = (s32[]{:T(128)}, bf16[2,385]{1,0:T(2,128)(2,1)S(1)}, s32[2,2]{1,0:T(2,128)S(1)}, bf16[2,63]{1,0:T(2,128)(2,1)S(1)}, s32[]{:T(128)}, /*index=5*/s32[2]{0:T(128)}) while((s32[]{:T(128)}, bf16[2,385]{1,0:T(2,128)(2,1)S(1)}, s32[2,2]{1,0:T(2,128)S(1)}, bf16[2,63]{1,0:T(2,128)(2,1)S(1)}, s32[]{:T(128)}, /*index=5*/s32[2]{0:T(128)}) %tuple.80), condition=%wide.while_cond.2, body=%wide.while_body.2.sunk | while | flops 74 | bytes 769 | solution.py:27
  29.8 0.6 fusion.60
  30.4 2.6 %and_reduce_fusion.10 = pred[]{:T(512)} fusion(s32[2]{0:T(128)} %get-tuple-element.268, s32[1]{0:T(128)} %bitcast.137, s32[1]{0:T(128)} %bitcast.138), kind=kLoop, calls=%fused_computation.6.clone.1 | loop fusion | flops 9 | bytes 17 | tf_op jit(solution)/shard_map/vmap(vmap())/scatter
  33.0 1.9 %broadcast_select_fusion.10 = bf16[1,63]{1,0:T(2,128)(2,1)S(1)} fusion(pred[]{:T(512)} %and_reduce_fusion.10, bf16[2,63]{1,0:T(2,128)(2,1)S(1)} %get-tuple-element.266, s32[]{:T(128)} %get-tuple-element.257, bf16[2,385]{1,0:T(2,128)(2,1)S(1)} %get-tuple-element.258, s32[]{:T(128)} %bitcast.139, s32[]{:T(128)} %bitcast.140), kind=kLoop, calls=%fused_computation.7.clone.1 | loop fusion | flops 63 | bytes 391 | tf_op jit(solution)/shard_map/vmap(vmap())/scatter
  34.9 1.6 dynamic-update-slice.10
  36.5 0.6 fusion.60
  37.1 2.6 %and_reduce_fusion.10 = pred[]{:T(512)} fusion(s32[2]{0:T(128)} %get-tuple-element.268, s32[1]{0:T(128)} %bitcast.137, s32[1]{0:T(128)} %bitcast.138), kind=kLoop, calls=%fused_computation.6.clone.1 | loop fusion | flops 9 | bytes 17 | tf_op jit(solution)/shard_map/vmap(vmap())/scatter
  39.7 1.9 %broadcast_select_fusion.10 = bf16[1,63]{1,0:T(2,128)(2,1)S(1)} fusion(pred[]{:T(512)} %and_reduce_fusion.10, bf16[2,63]{1,0:T(2,128)(2,1)S(1)} %get-tuple-element.266, s32[]{:T(128)} %get-tuple-element.257, bf16[2,385]{1,0:T(2,128)(2,1)S(1)} %get-tuple-element.258, s32[]{:T(128)} %bitcast.139, s32[]{:T(128)} %bitcast.140), kind=kLoop, calls=%fused_computation.7.clone.1 | loop fusion | flops 63 | bytes 391 | tf_op jit(solution)/shard_map/vmap(vmap())/scatter
  41.7 1.6 dynamic-update-slice.10
  43.3 13.6 %while.7 = (s32[]{:T(128)}, bf16[2,385]{1,0:T(2,128)(2,1)S(1)}, s32[2,2]{1,0:T(2,128)S(1)}, bf16[2,63]{1,0:T(2,128)(2,1)S(1)}, s32[]{:T(128)}, /*index=5*/s32[2]{0:T(128)}) while((s32[]{:T(128)}, bf16[2,385]{1,0:T(2,128)(2,1)S(1)}, s32[2,2]{1,0:T(2,128)S(1)}, bf16[2,63]{1,0:T(2,128)(2,1)S(1)}, s32[]{:T(128)}, /*index=5*/s32[2]{0:T(128)}) %tuple.89), condition=%wide.while_cond.3, body=%wide.while_body.3.sunk | while | flops 74 | bytes 769 | solution.py:27
  43.3 0.6 fusion.61
  43.9 2.6 %and_reduce_fusion.11 = pred[]{:T(512)} fusion(s32[2]{0:T(128)} %get-tuple-element.286, s32[1]{0:T(128)} %bitcast.141, s32[1]{0:T(128)} %bitcast.142), kind=kLoop, calls=%fused_computation.9.clone.1 | loop fusion | flops 9 | bytes 17 | tf_op jit(solution)/shard_map/vmap(vmap())/scatter
  46.5 2.0 %broadcast_select_fusion.11 = bf16[1,63]{1,0:T(2,128)(2,1)S(1)} fusion(pred[]{:T(512)} %and_reduce_fusion.11, bf16[2,63]{1,0:T(2,128)(2,1)S(1)} %get-tuple-element.284, s32[]{:T(128)} %get-tuple-element.275, bf16[2,385]{1,0:T(2,128)(2,1)S(1)} %get-tuple-element.276, s32[]{:T(128)} %bitcast.143, s32[]{:T(128)} %bitcast.144), kind=kLoop, calls=%fused_computation.10.clone.1 | loop fusion | flops 63 | bytes 391 | tf_op jit(solution)/shard_map/vmap(vmap())/scatter
  48.5 1.5 dynamic-update-slice.11
  50.1 0.6 fusion.61
  50.7 2.6 %and_reduce_fusion.11 = pred[]{:T(512)} fusion(s32[2]{0:T(128)} %get-tuple-element.286, s32[1]{0:T(128)} %bitcast.141, s32[1]{0:T(128)} %bitcast.142), kind=kLoop, calls=%fused_computation.9.clone.1 | loop fusion | flops 9 | bytes 17 | tf_op jit(solution)/shard_map/vmap(vmap())/scatter
  53.4 2.0 %broadcast_select_fusion.11 = bf16[1,63]{1,0:T(2,128)(2,1)S(1)} fusion(pred[]{:T(512)} %and_reduce_fusion.11, bf16[2,63]{1,0:T(2,128)(2,1)S(1)} %get-tuple-element.284, s32[]{:T(128)} %get-tuple-element.275, bf16[2,385]{1,0:T(2,128)(2,1)S(1)} %get-tuple-element.276, s32[]{:T(128)} %bitcast.143, s32[]{:T(128)} %bitcast.144), kind=kLoop, calls=%fused_computation.10.clone.1 | loop fusion | flops 63 | bytes 391 | tf_op jit(solution)/shard_map/vmap(vmap())/scatter
  55.3 1.5 dynamic-update-slice.11
  57.0 0.5 tile.19
  58.1 0.7 tile.41
  59.5 1.9 %collective-permute-start = (bf16[63,1024]{1,0:T(8,128)(2,1)S(1)}, bf16[63,1024]{1,0:T(8,128)(2,1)S(1)}, u32[]{:S(2)}, u32[]{:S(2)}) collective-permute-start(bf16[63,1024]{1,0:T(8,128)(2,1)S(1)} %bitcast.162), channel_id=1, source_target_pairs={{0,8},{8,16},{16,24},{24,32},{32,40},{40,48},{48,56},{56,64},{64,7... | collective-permute-start | bytes 387080 | tf_op jit(solution)/shard_map/ppermute | solution.py:19
  61.6 5.1 %collective-permute-start.1 = (bf16[63,1024]{1,0:T(8,128)(2,1)S(1)}, bf16[63,1024]{1,0:T(8,128)(2,1)S(1)}, u32[]{:S(2)}, u32[]{:S(2)}) collective-permute-start(bf16[63,1024]{1,0:T(8,128)(2,1)S(1)} %bitcast.163), channel_id=1, source_target_pairs={{8,0},{16,8},{24,16},{32,24},{40,32},{48,40},{56,48},{64,56},{72,6... | collective-permute-start | bytes 387080 | tf_op jit(solution)/shard_map/ppermute | solution.py:20
  67.8 1.5 collective-permute-done.1
  72.0 1.0 fusion.41
  73.0 5.2 %collective-permute-start.2 = (bf16[2,63,1024]{1,2,0:T(8,128)(2,1)}, bf16[2,63,1024]{1,2,0:T(8,128)(2,1)S(1)}, u32[]{:S(2)}, u32[]{:S(2)}) collective-permute-start(bf16[2,63,1024]{1,2,0:T(8,128)(2,1)} %get-tuple-element.83), channel_id=1, source_target_pairs={{0,8},{8,16},{16,24},{24,32},{32,40},{40,48},{48,56},{56,64},{64,7... | collective-permute-start | bytes 774152 | tf_op jit(solution)/shard_map/ppermute | solution.py:19
  78.2 2.2 %collective-permute-start.3 = (bf16[2,63,1024]{1,2,0:T(8,128)(2,1)S(1)}, bf16[2,63,1024]{1,2,0:T(8,128)(2,1)}, u32[]{:S(2)}, u32[]{:S(2)}) collective-permute-start(bf16[2,63,1024]{1,2,0:T(8,128)(2,1)S(1)} %get-tuple-element.84), channel_id=1, source_target_pairs={{8,0},{16,8},{24,16},{32,24},{40,32},{48,40},{56,48},{64,56},{72,6... | collective-permute-start | bytes 774152 | tf_op jit(solution)/shard_map/ppermute | solution.py:20
  80.4 12.3 %while.4 = (s32[]{:T(128)}, bf16[2,255]{1,0:T(2,128)(2,1)S(1)}, s32[2,2]{1,0:T(2,128)S(1)}, bf16[2,63]{1,0:T(2,128)(2,1)S(1)}, s32[]{:T(128)}, /*index=5*/s32[2]{0:T(128)S(1)}) while((s32[]{:T(128)}, bf16[2,255]{1,0:T(2,128)(2,1)S(1)}, s32[2,2]{1,0:T(2,128)S(1)}, bf16[2,63]{1,0:T(2,128)(2,1)S(1)}, s32[]{:T(128)}, /*index=5*/s32[2]{0:T(128)S(1)}) %tuple.88), condition=%wide.while_cond, body=%wide.while_body.sunk | while | flops 74 | bytes 769 | solution.py:27
  80.4 0.6 fusion.58
  81.1 2.0 %and_reduce_fusion.8 = pred[]{:T(512)} fusion(s32[2]{0:T(128)S(1)} %get-tuple-element.232, s32[1]{0:T(128)} %bitcast.129, s32[1]{0:T(128)} %bitcast.130), kind=kLoop, calls=%fused_computation.clone.1 | loop fusion | flops 9 | bytes 17 | tf_op jit(solution)/shard_map/vmap(vmap())/scatter
  83.1 2.0 %broadcast_select_fusion.8 = bf16[1,63]{1,0:T(2,128)(2,1)S(1)} fusion(pred[]{:T(512)} %and_reduce_fusion.8, bf16[2,63]{1,0:T(2,128)(2,1)S(1)} %get-tuple-element.230, s32[]{:T(128)} %get-tuple-element.221, bf16[2,255]{1,0:T(2,128)(2,1)S(1)} %get-tuple-element.222, s32[]{:T(128)} %bitcast.131, s32[]{:T(128)} %bitcast.132), kind=kLoop, calls=%fused_computation.1.clone.1 | loop fusion | flops 63 | bytes 391 | tf_op jit(solution)/shard_map/vmap(vmap())/scatter
  85.0 1.6 dynamic-update-slice.8
  86.6 0.6 fusion.58
  87.2 2.0 %and_reduce_fusion.8 = pred[]{:T(512)} fusion(s32[2]{0:T(128)S(1)} %get-tuple-element.232, s32[1]{0:T(128)} %bitcast.129, s32[1]{0:T(128)} %bitcast.130), kind=kLoop, calls=%fused_computation.clone.1 | loop fusion | flops 9 | bytes 17 | tf_op jit(solution)/shard_map/vmap(vmap())/scatter
  89.2 2.0 %broadcast_select_fusion.8 = bf16[1,63]{1,0:T(2,128)(2,1)S(1)} fusion(pred[]{:T(512)} %and_reduce_fusion.8, bf16[2,63]{1,0:T(2,128)(2,1)S(1)} %get-tuple-element.230, s32[]{:T(128)} %get-tuple-element.221, bf16[2,255]{1,0:T(2,128)(2,1)S(1)} %get-tuple-element.222, s32[]{:T(128)} %bitcast.131, s32[]{:T(128)} %bitcast.132), kind=kLoop, calls=%fused_computation.1.clone.1 | loop fusion | flops 63 | bytes 391 | tf_op jit(solution)/shard_map/vmap(vmap())/scatter
  91.2 1.6 dynamic-update-slice.8
  92.8 0.7 tile.43
  94.8 0.8 copy-done.3
  95.6 2.2 %pad_maximum_fusion = bf16[2,382,1024]{1,2,0:T(8,128)(2,1)S(1)} fusion(bf16[2,63,1024]{1,2,0:T(8,128)(2,1)} %collective-permute-done.3, bf16[2,256,1024]{1,2,0:T(8,128)(2,1)S(1)} %fusion.3, bf16[2,63,1024]{1,2,0:T(8,128)(2,1)} %copy-done.3), kind=kLoop, calls=%fused_computation.26 | loop fusion | flops 4694016 | bytes 3129344 | tf_op jit(solution)/shard_map/concatenate | solution.py:21
  97.7 1.5 pad_slice_fusion.1
  99.2 2.9 %copy.54 = bf16[2,382,8,128]{3,2,1,0:T(8,128)(2,1)} copy(bf16[2,382,8,128]{1,3,2,0:T(8,128)(2,1)} %bitcast.149) | data formatting | bytes 3129344 | tf_op jit(solution)/shard_map/reshape | solution.py:42
  102.2 2.0 %copy.56 = bf16[2,382,8,128]{3,2,1,0:T(8,128)(2,1)} copy(bf16[2,382,8,128]{1,3,2,0:T(8,128)(2,1)S(1)} %bitcast.148) | data formatting | bytes 3129344 | tf_op jit(solution)/shard_map/reshape | solution.py:42
  104.2 3.7 %fusion.28 = f32[2,382,8,128]{3,2,1,0:T(8,128)} fusion(bf16[2,382,8,128]{3,2,1,0:T(8,128)(2,1)} %copy.54, bf16[2,128,384]{2,1,0:T(8,128)(2,1)S(1)} %bitcast.152), kind=kOutput, calls=%fused_computation.62 | convolution fusion | flops 200278016 | bytes 4759552 | tf_op jit(solution)/shard_map/srny,scy->srnc/dot_general | solution.py:46
  107.9 2.2 %fusion.27 = f32[2,382,8,128]{3,2,1,0:T(8,128)} fusion(bf16[2,382,8,128]{3,2,1,0:T(8,128)(2,1)S(1)} %copy-done.1, bf16[2,128,384]{2,1,0:T(8,128)(2,1)S(1)} %bitcast.153), kind=kOutput, calls=%fused_computation.59 | convolution fusion | flops 200278016 | bytes 4759552 | tf_op jit(solution)/shard_map/srny,scy->srnc/dot_general | solution.py:46
  110.1 1.2 copy.55
  111.4 4.7 %add_convert_fusion = bf16[2,382,8,128]{3,2,1,0:T(8,128)(2,1)} fusion(f32[2,382,8,128]{3,2,1,0:T(8,128)} %fusion.27, f32[2,382,8,128]{3,2,1,0:T(8,128)} %fusion.28, bf16[2,382,8,128]{3,2,1,0:T(8,128)(2,1)S(1)} %copy.55, bf16[2,128,384]{2,1,0:T(8,128)(2,1)S(1)} %bitcast.154), kind=kOutput, calls=%fused_computation.14 | convolution fusion | flops 202625024 | bytes 9453568 | tf_op jit(solution)/shard_map/srny,scy->srnc/dot_general | solution.py:46
  116.0 2.1 %copy.57 = bf16[2,382,8,128]{1,3,2,0:T(8,128)(2,1)S(1)} copy(bf16[2,382,8,128]{3,2,1,0:T(8,128)(2,1)} %add_convert_fusion) | data formatting | bytes 3129344 | tf_op jit(solution)/shard_map/convert_element_type | solution.py:113
  119.4 1.0 copy.66
  120.5 53.0 %reduce-scatter.4.cloned.1.call-done = bf16[128,256]{1,0:T(8,128)(2,1)} async-done(((bf16[1024,256]{1,0:T(8,128)(2,1)}), bf16[128,256]{1,0:T(8,128)(2,1)}) %reduce-scatter.4.cloned.1.call-update) | async-done | bytes 65552
  173.5 0.9 copy.67
  174.4 0.7 fusion.26
  (81 shorter events, 8.4 us)
Async XLA Ops:
  6.5 7.0 %copy-start = (s32[16,2]{0,1:T(2,128)S(1)}, s32[16,2]{0,1:T(2,128)}, u32[]{:S(2)}) copy-start(s32[16,2]{0,1:T(2,128)} %param.11) | copy-start | bytes 388
  8.3 50.7 %copy-start.2 = (bf16[256,1024]{1,0:T(8,128)(2,1)S(1)}, bf16[256,1024]{1,0:T(8,128)(2,1)}, u32[]{:S(2)}) copy-start(bf16[256,1024]{1,0:T(8,128)(2,1)} %param.9) | copy-start | bytes 1572868
  8.3 51.1 %all-to-all-start = ((bf16[8,256,128]{2,1,0:T(8,128)(2,1)}), bf16[8,256,128]{2,1,0:T(8,128)(2,1)S(1)}, u32[]{:S(2)}, u32[]{:S(2)}) async-start(bf16[8,256,128]{2,1,0:T(8,128)(2,1)} %stack.2), calls=%async_computation | async-start | bytes 1048576 | tf_op jit(solution)/shard_map/all_to_all | solution.py:106
  13.5 160.0 %reduce-scatter.4.cloned.1.call-start = ((), (), s32[]{:S(2)}) async-start(), calls=%async_computation.2 | async-start | bytes 589824
  43.2 15.9 %copy-start.7 = (f32[4]{0:T(128)S(1)}, f32[4]{0:T(128)}, u32[]{:S(2)}) copy-start(f32[4]{0:T(128)} %param.13) | copy-start | bytes 52
  59.5 7.8 %collective-permute-start = (bf16[63,1024]{1,0:T(8,128)(2,1)S(1)}, bf16[63,1024]{1,0:T(8,128)(2,1)S(1)}, u32[]{:S(2)}, u32[]{:S(2)}) collective-permute-start(bf16[63,1024]{1,0:T(8,128)(2,1)S(1)} %bitcast.162), channel_id=1, source_target_pairs={{0,8},{8,16},{16,24},{24,32},{32,40},{40,48},{48,56},{56,64},{64,7... | collective-permute-start | bytes 387080 | tf_op jit(solution)/shard_map/ppermute | solution.py:19
  61.6 7.7 %collective-permute-start.1 = (bf16[63,1024]{1,0:T(8,128)(2,1)S(1)}, bf16[63,1024]{1,0:T(8,128)(2,1)S(1)}, u32[]{:S(2)}, u32[]{:S(2)}) collective-permute-start(bf16[63,1024]{1,0:T(8,128)(2,1)S(1)} %bitcast.163), channel_id=1, source_target_pairs={{8,0},{16,8},{24,16},{32,24},{40,32},{48,40},{56,48},{64,56},{72,6... | collective-permute-start | bytes 387080 | tf_op jit(solution)/shard_map/ppermute | solution.py:20
  72.0 8.5 %copy-start.6 = (s32[2]{0:T(128)S(1)}, s32[2]{0:T(128)}, u32[]{:S(2)}) copy-start(s32[2]{0:T(128)} %get-tuple-element.298) | copy-start | bytes 28
  73.0 21.7 %collective-permute-start.2 = (bf16[2,63,1024]{1,2,0:T(8,128)(2,1)}, bf16[2,63,1024]{1,2,0:T(8,128)(2,1)S(1)}, u32[]{:S(2)}, u32[]{:S(2)}) collective-permute-start(bf16[2,63,1024]{1,2,0:T(8,128)(2,1)} %get-tuple-element.83), channel_id=1, source_target_pairs={{0,8},{8,16},{16,24},{24,32},{32,40},{40,48},{48,56},{56,64},{64,7... | collective-permute-start | bytes 774152 | tf_op jit(solution)/shard_map/ppermute | solution.py:19
  78.2 17.4 %collective-permute-start.3 = (bf16[2,63,1024]{1,2,0:T(8,128)(2,1)S(1)}, bf16[2,63,1024]{1,2,0:T(8,128)(2,1)}, u32[]{:S(2)}, u32[]{:S(2)}) collective-permute-start(bf16[2,63,1024]{1,2,0:T(8,128)(2,1)S(1)} %get-tuple-element.84), channel_id=1, source_target_pairs={{8,0},{16,8},{24,16},{32,24},{40,32},{48,40},{56,48},{64,56},{72,6... | collective-permute-start | bytes 774152 | tf_op jit(solution)/shard_map/ppermute | solution.py:20
  94.8 0.8 copy-start.3
  104.2 3.7 %copy-start.1 = (bf16[2,382,8,128]{3,2,1,0:T(8,128)(2,1)S(1)}, bf16[2,382,8,128]{3,2,1,0:T(8,128)(2,1)}, u32[]{:S(2)}) copy-start(bf16[2,382,8,128]{3,2,1,0:T(8,128)(2,1)} %copy.56) | copy-start | bytes 4694020
  119.1 55.3 %copy-start.4 = (bf16[256,128]{1,0:T(8,128)(2,1)S(1)}, bf16[256,128]{1,0:T(8,128)(2,1)}, u32[]{:S(2)}) copy-start(bf16[256,128]{1,0:T(8,128)(2,1)} %param.8) | copy-start | bytes 196612
  119.1 55.3 %copy-start.5 = (s32[256,128]{1,0:T(8,128)S(1)}, s32[256,128]{1,0:T(8,128)}, u32[]{:S(2)}) copy-start(s32[256,128]{1,0:T(8,128)} %param.10) | copy-start | bytes 393220
Sparse Core Ops, SparseCore 0:
  120.6 52.8 reduce-scatter.3
